TPU v7x, 512 devices: a whole 4x8x8 slice. The times are simulated.
512 devices in a mesh: stream: 8 (over y), span: 16 (over z, core), vert: 4 (over x).
Axes of the slice: x: 4, y: 8, z: 8, core: 2. Of those that a mesh axis runs over, the one named last changes fastest.
Arguments:
- fields: float32 [5, 128, 256, 1024], P(None, 'vert', 'span', 'stream'), may hold values from -6 to 6
- solid_frac: float32 [128, 256, 1024], P('vert', 'span', 'stream'), may hold values from 0 to 1
- panels: float32 [32768, 5, 256], P(('stream', 'span', 'vert')), may hold values from -0.015625 to 0.015625
- panel_owner: int32 [32768, 1], P(('stream', 'span', 'vert')), may hold values from 0 to 63; in each aligned block of 64 rows (0 to 63, 64 to 127, ...) at most 2 rows name the same one
- deck_cells: int32 [4, 16, 8, 2048], P('vert', 'span', 'stream'), may hold values from 0 to 65535
- deck_geom: float32 [4, 16, 8, 3, 2048], P('vert', None, 'stream'), may hold values from -6 to 6
- strip_ids: int32 [4, 16, 8, 2048], P('vert', None, 'stream'), may hold values from 0 to 63, as said below
- mode_shapes: float32 [3, 64, 32], replicated, may hold values from -0.0034179688 to 0.0034179688
Outputs:
- new_fields: float32 [5, 128, 256, 1024], P(None, 'vert', 'span', 'stream')
- modal_force: float32 [32], replicated
Inputs may be any that keep to these rules, and one draw needn't show every extreme that they name: `panel_owner`: tile number s * 4 + v for along-deck tile s and vertical tile v. Among the 64 panels of one device no tile is named more than 2 times; some device names some tile exactly 2 times. `strip_ids`: cells of along-deck tile s belong to strips s * 4 to (s + 1) * 4 - 1.
All inputs are finite; a program needn't handle non-finite values.
Results may differ from a plain program's by a relative error of at most 0.00012.
Values sent between devices are 32-bit elements; how exact they have to be, the bound alone decides.
No kernel may reach another device: no remote copies, remote signals or barrier semaphores. Data moves between devices by JAX's collectives and lax.ppermute only.
A program may use at most 128 MiB of HBM per device.

v0:
```python
import math
import jax
import jax.numpy as jnp
from jax import lax
from jax.sharding import PartitionSpec as P

CAP = 2
time_step = 0.15
viscous = 0.05
heat_diff = 0.03
sound_sq = 1.0
buoyant = 0.5
penalty = 0.5
relax_time = 0.5
relax_depth = 8.0
wave_cols = 16


def extended(block, sides, width):
    for axis, dim in sides:
        count = lax.axis_size(axis)
        forward = [(i, i + 1) for i in range(count - 1)]
        backward = [(target, source) for source, target in forward]
        low = lax.ppermute(
            lax.slice_in_dim(block, block.shape[dim] - width, None, axis=dim), axis, forward
        )
        high = lax.ppermute(lax.slice_in_dim(block, 0, width, axis=dim), axis, backward)
        block = jnp.concatenate([low, block, high], axis=dim)
    return block


def wave_basis(heights, widths, total_z, total_y, spec):
    modes = jnp.arange(spec, dtype=jnp.int32)
    across = (modes % wave_cols)[:, None, None]
    upward = (modes // wave_cols)[:, None, None]
    period = total_y * total_z
    phase = (
        across * widths[None, None, :] * total_z + upward * heights[None, :, None] * total_y
    ) % period
    angle = phase.astype(jnp.float32) * (2.0 * math.pi / period)
    return jnp.concatenate([jnp.cos(angle), jnp.sin(angle)], axis=0)


def relax_weights(positions, limit):
    spots = positions.astype(jnp.float32)
    return jnp.where(positions < limit, jnp.exp(-spots / relax_depth) / relax_time, 0.0)


def rates(padded, solid_frac, relax_rate, target_plane):
    centre = padded[:, 1:-1, 1:-1, 1:-1]
    east_side = padded[:, 1:-1, 1:-1, 2:]
    west_side = padded[:, 1:-1, 1:-1, :-2]
    north_side = padded[:, 1:-1, 2:, 1:-1]
    south_side = padded[:, 1:-1, :-2, 1:-1]
    upper_side = padded[:, 2:, 1:-1, 1:-1]
    lower_side = padded[:, :-2, 1:-1, 1:-1]
    grad_x = 0.5 * (east_side - west_side)
    grad_y = 0.5 * (north_side - south_side)
    grad_z = 0.5 * (upper_side - lower_side)
    laplace = (
        east_side + west_side + north_side + south_side + upper_side + lower_side - 6.0 * centre
    )
    speed_x = centre[0]
    speed_y = centre[1]
    speed_z = centre[2]
    carried = speed_x * grad_x + speed_y * grad_y + speed_z * grad_z
    coeffs = jnp.array([viscous, viscous, viscous, viscous, heat_diff], jnp.float32)[
        :, None, None, None
    ]
    damping = solid_frac / penalty
    nudging = relax_rate[None, None, None, :] * (target_plane[:, :, :, None] - centre)
    common = coeffs * laplace - carried + nudging
    extra_terms = jnp.stack(
        [
            -grad_x[3] - damping * speed_x,
            -grad_y[3] - damping * speed_y,
            -grad_z[3] - damping * speed_z + buoyant * centre[4],
            -sound_sq * (grad_x[0] + grad_y[1] + grad_z[2]),
            jnp.zeros_like(speed_x),
        ]
    )
    return common + extra_terms


def pack_slots(flat_panels, target_tile, chosen, tile_count):
    running = jnp.cumsum(chosen, axis=0) - 1
    slot_rank = jnp.sum(chosen * running, axis=1)
    slot_index = target_tile * CAP + slot_rank
    dispatch = (
        slot_index[None, :] == jnp.arange(tile_count * CAP, dtype=jnp.int32)[:, None]
    ).astype(jnp.float32)
    return jnp.dot(dispatch, flat_panels, precision=lax.Precision.HIGHEST)


def strip_forces(traction, labels, strip_count):
    columns = jnp.arange(strip_count, dtype=jnp.int32)

    def add_row(running, item_pair):
        row_values, row_labels = item_pair
        member = (row_labels[:, None] == columns[None, :]).astype(jnp.float32)
        return (running + jnp.dot(row_values, member, precision=lax.Precision.HIGHEST), None)

    start_value = jnp.zeros((traction.shape[1], strip_count), jnp.float32)
    summed, ignored = lax.scan(add_row, start_value, (traction, labels))
    return summed


def on_device(
    fields, solid_frac, panels, panel_owner, deck_cells, deck_geom, strip_ids, mode_shapes
):
    depth_cells = fields.shape[1]
    span_cells = fields.shape[2]
    wind_cells = fields.shape[3]
    n_span = lax.axis_size("span")
    n_vert = lax.axis_size("vert")
    stream_pos = lax.axis_index("stream")
    span_pos = lax.axis_index("span")
    vert_pos = lax.axis_index("vert")
    tile_count = n_span * n_vert
    held_panels = panels.shape[0]
    spec_cols = panels.shape[2]
    flat_panels = panels.reshape(held_panels, 5 * spec_cols)
    target_tile = panel_owner[:, 0]
    chosen = (target_tile[:, None] == jnp.arange(tile_count, dtype=jnp.int32)[None, :]).astype(
        jnp.int32
    )
    outgoing = pack_slots(flat_panels, target_tile, chosen, tile_count)
    arrived = lax.all_to_all(
        outgoing.reshape(tile_count, CAP * 5 * spec_cols),
        ("span", "vert"),
        split_axis=0,
        concat_axis=0,
        tiled=True,
    )
    coeffs = jnp.sum(arrived.reshape(-1, 5 * spec_cols), axis=0)
    coeffs = coeffs.reshape(5, spec_cols)
    heights = vert_pos * depth_cells + jnp.arange(depth_cells, dtype=jnp.int32)
    widths = span_pos * span_cells + jnp.arange(span_cells, dtype=jnp.int32)
    wave_table = wave_basis(
        heights, widths, depth_cells * n_vert, span_cells * n_span, spec_cols // 2
    )
    wave_table = wave_table.reshape(spec_cols, depth_cells * span_cells)
    partial_value = jnp.dot(coeffs, wave_table, precision=lax.Precision.HIGHEST)
    inflow_plane = lax.psum(partial_value, "stream").reshape(5, depth_cells, span_cells)
    target_plane = inflow_plane + jnp.array([1.0, 0.0, 0.0, 0.0, 0.0], jnp.float32)[:, None, None]
    wind_first = stream_pos * wind_cells
    relax_rate = relax_weights(
        wind_first + jnp.arange(wind_cells, dtype=jnp.int32), wind_cells // 2
    )

    def advance(state):
        padded = extended(state, (("stream", 3), ("span", 2), ("vert", 1)), 1)
        return rates(padded, solid_frac, relax_rate, target_plane)

    first_update = fields + time_step * advance(fields)
    second_rate = advance(first_update)
    new_fields = 0.5 * (fields + first_update + time_step * second_rate)
    pressure = new_fields[3].reshape(-1)
    sampled = pressure[deck_cells[0, 0, 0]]
    strip_count = mode_shapes.shape[1]
    rows_all = lax.all_gather(sampled.reshape(1, 1, 1, -1), "span", axis=1, tiled=True)
    traction = rows_all[0, :, 0][:, None, :] * deck_geom[0, :, 0]
    forces = strip_forces(traction, strip_ids[0, :, 0], strip_count)
    modal_part = jnp.einsum("cj,cjm->m", forces, mode_shapes, precision=lax.Precision.HIGHEST)
    modal_force = lax.psum(modal_part, ("stream", "vert"))
    return (new_fields, modal_force)


def solution(mesh):
    return jax.shard_map(
        on_device,
        mesh=mesh,
        in_specs=(
            P(None, "vert", "span", "stream"),
            P("vert", "span", "stream"),
            P(("stream", "span", "vert"), None, None),
            P(("stream", "span", "vert"), None),
            P("vert", "span", "stream", None),
            P("vert", None, "stream", None, None),
            P("vert", None, "stream", None),
            P(),
        ),
        out_specs=(P(None, "vert", "span", "stream"), P()),
        check_vma=False,
    )
```

profile of v0, /device:TPU:64, one launch (start us, length us, event | category | flops | bytes accessed | tf_op | source)
XLA Modules:
  0.0 263.3 jit_solution(5278629360200519969)
XLA Ops:
  0.6 2.2 fusion.52
  3.4 1.3 collective-permute-start
  5.3 4.5 %collective-permute-start.1 = (f32[5,32,16,1]{1,2,3,0:T(8,128)S(1)}, f32[5,32,16,1]{1,2,3,0:T(8,128)S(1)}, u32[]{:S(2)}, u32[]{:S(2)}) collective-permute-start(f32[5,32,16,1]{1,2,3,0:T(8,128)S(1)} %copy.56), channel_id=1, source_target_pairs={{0,64},{64,128},{128,192},{192,256},{256,320},{320,384},{384,448},... | collective-permute-start | bytes 30728 | tf_op jit(solution)/shard_map/ppermute | solution.py:24
  10.7 1.5 all_to_all.8
  12.2 13.3 %all-to-all-start = ((f32[64,1,2560]{2,1,0:T(1,128)}), f32[64,1,2560]{2,1,0:T(1,128)}, u32[]{:S(2)}, u32[]{:S(2)}) async-start(f32[64,1,2560]{2,1,0:T(1,128)} %all_to_all.8), calls=%async_computation | async-start | bytes 1310720 | tf_op jit(solution)/shard_map/all_to_all | solution.py:128
  25.6 0.9 bitcast_multiply_fusion.6
  26.7 1.7 fusion.46
  29.1 1.6 copy.39
  30.7 2.5 pad_maximum_fusion.39
  33.2 2.0 collective-permute-start.2
  35.2 2.3 collective-permute-start.3
  37.5 4.0 %collective-permute-done.2 = f32[5,32,1,130]{3,2,1,0:T(1,128)S(1)} collective-permute-done((f32[5,32,1,130]{3,2,1,0:T(1,128)S(1)}, f32[5,32,1,130]{3,2,1,0:T(1,128)S(1)}, u32[]{:S(2)}, u32[]{:S(2)}) %collective-permute-start.2) | collective-permute-done | bytes 83232 | tf_op jit(solution)/shard_map/ppermute | solution.py:27
  41.5 1.5 collective-permute-done.3
  43.2 1.3 collective-permute-start.4
  44.5 4.7 %collective-permute-start.5 = (f32[5,1,18,130]{3,2,1,0:T(8,128)S(1)}, f32[5,1,18,130]{3,2,1,0:T(8,128)S(1)}, u32[]{:S(2)}, u32[]{:S(2)}) collective-permute-start(f32[5,1,18,130]{3,2,1,0:T(8,128)S(1)} %get-tuple-element.71), channel_id=1, source_target_pairs={{0,1},{1,2},{2,3},{4,5},{5,6},{6,7},{8,9},{9,10},{10,11},{12,13},{... | collective-permute-start | bytes 140408 | tf_op jit(solution)/shard_map/ppermute | solution.py:24
  49.3 1.1 broadcast_multiply_fusion.4
  50.5 1.2 collective-permute-done.5
  51.7 3.2 %broadcast_multiply_fusion.3 = (f32[5,32,16,128]{3,2,1,0:T(8,128)S(1)}, f32[5,32,16,128]{3,2,1,0:T(8,128)S(1)}) fusion(f32[5,1,18,130]{3,2,1,0:T(8,128)S(1)} %collective-permute-done.4, f32[5,32,1,130]{3,2,1,0:T(1,128)S(1)} %collective-permute-done.2, f32[5,32,16,1]{3,2,1,0:T(8,128)S(1)} %copy.37, f32[5,32,16,128]{3,2,1,0:T(8,128)S(1)} %copy-done.1, ...), kind=kLoop, calls=%fused_computation.50 | loop fusion | flops 5242880 | bytes 4212640 | tf_op jit(solution)/shard_map/mul | solution.py:59
  54.9 0.7 fusion.40
  55.7 0.8 fusion.36
  56.4 0.8 fusion.32
  57.2 0.8 fusion.27
  58.7 2.6 %reduce = f32[64,2560]{1,0:T(8,128)S(1)} reduce(f32[64,1,2560]{2,1,0:T(1,128)} %all-to-all-done, f32[]{:T(128)} %constant.123), dimensions={1}, to_apply=%all_to_all.7.reduce_sub_computation | reduce | bytes 1310724 | tf_op jit(solution)/shard_map/all_to_all | solution.py:128
  61.5 1.5 fusion.3
  63.1 30.8 %psum.14 = f32[5,32,16]{2,1,0:T(8,128)S(1)} all-reduce(f32[5,32,16]{2,1,0:T(8,128)S(1)} %reshape.200), channel_id=1, replica_groups=mesh['stream'=8,'span'=16,'vert'=4] {'stream'}, use_global_device_ids=true, to_apply=%region_3.4 | all-reduce | flops 2560 | bytes 20480 | tf_op jit(solution)/shard_map/psum | solution.py:144
  94.0 7.5 %multiply_add_fusion = f32[5,32,16,128]{3,2,1,0:T(8,128)S(1)} fusion(f32[5,32,16,128]{3,2,1,0:T(8,128)S(1)} %copy-done.1, f32[5,32,16,128]{3,2,1,0:T(8,128)} %broadcast_dynamic-update-slice_fusion.1, f32[5,32,16]{2,1,0:T(8,128)S(1)} %broadcast_add_fusion.1, f32[128]{0:T(128)S(1)} %compare_select_fusion.1, f32[32,16,128]{2,1,0:T(8,128)} %get-tuple-element.87, ...), kind=kLoop, calls=%fused_computation.45 | loop fusion | flops 13434880 | bytes 5009844 | tf_op jit(solution)/shard_map/add | solution.py:155
  101.5 1.9 fusion.51
  103.5 1.9 copy.44
  105.4 1.3 collective-permute-start.6
  106.7 1.9 copy.46
  108.5 4.5 %collective-permute-start.7 = (f32[5,32,16,1]{1,2,3,0:T(8,128)S(1)}, f32[5,32,16,1]{1,2,3,0:T(8,128)S(1)}, u32[]{:S(2)}, u32[]{:S(2)}) collective-permute-start(f32[5,32,16,1]{1,2,3,0:T(8,128)S(1)} %copy.46), channel_id=1, source_target_pairs={{0,64},{64,128},{128,192},{192,256},{256,320},{320,384},{384,448},... | collective-permute-start | bytes 30728 | tf_op jit(solution)/shard_map/ppermute | solution.py:24
  113.2 1.6 copy.45
  114.8 1.6 copy.47
  116.4 2.9 %pad_maximum_fusion.36 = (f32[5,32,1,130]{3,2,1,0:T(1,128)S(1)}, f32[5,32,1,130]{3,2,1,0:T(1,128)S(1)}) fusion(f32[5,32,16,1]{3,2,1,0:T(8,128)} %copy.45, f32[5,32,16,128]{3,2,1,0:T(8,128)S(1)} %multiply_add_fusion, f32[5,32,16,1]{3,2,1,0:T(8,128)} %copy.47), kind=kLoop, calls=%fused_computation.118 | loop fusion | flops 83200 | bytes 1497600 | tf_op jit(solution)/shard_map/concatenate | solution.py:28
  119.3 2.1 collective-permute-start.8
  121.4 2.6 collective-permute-start.9
  124.2 3.8 %collective-permute-done.9 = f32[5,32,1,130]{3,2,1,0:T(1,128)S(1)} collective-permute-done((f32[5,32,1,130]{3,2,1,0:T(1,128)S(1)}, f32[5,32,1,130]{3,2,1,0:T(1,128)S(1)}, u32[]{:S(2)}, u32[]{:S(2)}) %collective-permute-start.9) | collective-permute-done | bytes 83232 | tf_op jit(solution)/shard_map/ppermute | solution.py:24
  128.2 1.3 collective-permute-start.10
  129.5 5.0 %collective-permute-start.11 = (f32[5,1,18,130]{3,2,1,0:T(8,128)S(1)}, f32[5,1,18,130]{3,2,1,0:T(8,128)S(1)}, u32[]{:S(2)}, u32[]{:S(2)}) collective-permute-start(f32[5,1,18,130]{3,2,1,0:T(8,128)S(1)} %get-tuple-element.69), channel_id=1, source_target_pairs={{0,1},{1,2},{2,3},{4,5},{5,6},{6,7},{8,9},{9,10},{10,11},{12,13},{... | collective-permute-start | bytes 140408 | tf_op jit(solution)/shard_map/ppermute | solution.py:24
  134.5 1.1 broadcast_multiply_fusion.1
  135.6 1.3 collective-permute-done.11
  136.9 3.1 %broadcast_multiply_fusion = (f32[5,32,16,128]{3,2,1,0:T(8,128)S(1)}, f32[5,32,16,128]{3,2,1,0:T(8,128)S(1)}) fusion(f32[5,1,18,130]{3,2,1,0:T(8,128)S(1)} %collective-permute-done.10, f32[5,32,1,130]{3,2,1,0:T(1,128)S(1)} %collective-permute-done.8, f32[5,32,16,1]{3,2,1,0:T(8,128)S(1)} %copy-done.4, f32[5,32,16,128]{3,2,1,0:T(8,128)S(1)} %multiply_add_fusion, ...), kind=kLoop, calls=%fused_computation.47 | loop fusion | flops 5242880 | bytes 4212640 | tf_op jit(solution)/shard_map/mul | solution.py:59
  140.4 5.0 %add_multiply_fusion = f32[5,32,16,128]{3,2,1,0:T(8,128)S(1)} fusion(f32[5,32,16,128]{3,2,1,0:T(8,128)S(1)} %broadcast_dynamic-update-slice_fusion, f32[5,32,16,128]{3,2,1,0:T(8,128)S(1)} %multiply_add_fusion, f32[5,32,16,128]{3,2,1,0:T(8,128)S(1)} %copy-done.1, f32[32,16,128]{2,1,0:T(8,128)S(1)} %get-tuple-element.82, ...), kind=kLoop, calls=%fused_computation.44 | loop fusion | flops 14090240 | bytes 6320564 | tf_op jit(solution)/shard_map/mul | solution.py:157
  145.4 1.0 copy-done.7
  146.5 11.8 %gather_fusion = f32[2048]{0:T(1024)S(1)} fusion(f32[65536]{0:T(1024)S(1)} %bitcast.150, s32[2048]{0:T(1024)S(1)} %broadcast_clamp_fusion), kind=kCustom, calls=%fused_computation | custom fusion | bytes 24576 | tf_op jit(solution)/shard_map/gather | solution.py:159
  158.2 16.8 %all-gather = f32[32768]{0:T(1024)S(1)} all-gather(f32[2048]{0:T(1024)S(1)} %gather_fusion), channel_id=2, replica_groups=mesh['stream'=8,'span'=16,'vert'=4] {'span'}, dimensions={0}, use_global_device_ids=true | all-gather | bytes 139264 | tf_op jit(solution)/shard_map/all_gather | solution.py:161
  175.2 10.6 %while.11 = (s32[]{:T(128)}, f32[3,64]{1,0:T(4,128)S(1)}, f32[16,3,2048]{2,0,1:T(8,128)S(1)}, s32[16,2048]{1,0:T(8,128)S(1)}, s32[]{:T(128)}, /*index=5*/s32[]{:T(128)}) while((s32[]{:T(128)}, f32[3,64]{1,0:T(4,128)S(1)}, f32[16,3,2048]{2,0,1:T(8,128)S(1)}, s32[16,2048]{1,0:T(8,128)S(1)}, s32[]{:T(128)}, /*index=5*/s32[]{:T(128)}) %tuple.46), condition=%wide.region_5.6_spmd.clone, body=%wide.region_4.5_spmd.clone.sunk | while | flops 4850051 | bytes 99927 | solution.py:104
  186.0 77.3 %psum.15 = f32[32]{0:T(128)} all-reduce(f32[32]{0:T(128)S(1)} %convolution_bitcast_fusion), channel_id=1, replica_groups=mesh['stream'=8,'span'=16,'vert'=4] {'stream','vert'}, use_global_device_ids=true, to_apply=%region_6.7 | all-reduce | flops 32 | bytes 256 | tf_op jit(solution)/shard_map/psum | solution.py:165
  (128 shorter events, 15.2 us)
Async XLA Ops:
  0.6 185.2 %copy-start = (f32[3,64,32]{1,2,0:T(8,128)S(1)}, f32[3,64,32]{1,2,0:T(8,128)}, u32[]{:S(2)}) copy-start(f32[3,64,32]{1,2,0:T(8,128)} %param.20) | copy-start | bytes 73732
  2.8 7.1 %copy-start.14 = (s32[64,1]{0,1:T(1,128)S(1)}, s32[64,1]{0,1:T(1,128)}, u32[]{:S(2)}) copy-start(s32[64,1]{0,1:T(1,128)} %param.16) | copy-start | bytes 772
  2.8 7.4 %copy-start.11 = (f32[64,5,256]{2,0,1:T(8,128)S(1)}, f32[64,5,256]{2,0,1:T(8,128)}, u32[]{:S(2)}) copy-start(f32[64,5,256]{2,0,1:T(8,128)} %param.15) | copy-start | bytes 983044
  3.4 25.0 %collective-permute-start = (f32[5,32,16,1]{1,2,3,0:T(8,128)S(1)}, f32[5,32,16,1]{1,2,3,0:T(8,128)S(1)}, u32[]{:S(2)}, u32[]{:S(2)}) collective-permute-start(f32[5,32,16,1]{1,2,3,0:T(8,128)S(1)} %copy.55), channel_id=1, source_target_pairs={{64,0},{128,64},{192,128},{256,192},{320,256},{384,320},{448,384},... | collective-permute-start | bytes 30728 | tf_op jit(solution)/shard_map/ppermute | solution.py:27
  5.3 23.7 %collective-permute-start.1 = (f32[5,32,16,1]{1,2,3,0:T(8,128)S(1)}, f32[5,32,16,1]{1,2,3,0:T(8,128)S(1)}, u32[]{:S(2)}, u32[]{:S(2)}) collective-permute-start(f32[5,32,16,1]{1,2,3,0:T(8,128)S(1)} %copy.56), channel_id=1, source_target_pairs={{0,64},{64,128},{128,192},{192,256},{256,320},{320,384},{384,448},... | collective-permute-start | bytes 30728 | tf_op jit(solution)/shard_map/ppermute | solution.py:24
  10.7 14.8 %copy-start.1 = (f32[5,32,16,128]{3,2,1,0:T(8,128)S(1)}, f32[5,32,16,128]{3,2,1,0:T(8,128)}, u32[]{:S(2)}) copy-start(f32[5,32,16,128]{3,2,1,0:T(8,128)} %param.13) | copy-start | bytes 3932164
  12.2 14.2 %copy-start.13 = (s32[1,1,1,2048]{3,2,1,0:T(1,128)S(1)}, s32[1,1,1,2048]{3,2,1,0:T(1,128)}, u32[]{:S(2)}) copy-start(s32[1,1,1,2048]{3,2,1,0:T(1,128)} %param.17) | copy-start | bytes 24580
  12.2 46.5 %all-to-all-start = ((f32[64,1,2560]{2,1,0:T(1,128)}), f32[64,1,2560]{2,1,0:T(1,128)}, u32[]{:S(2)}, u32[]{:S(2)}) async-start(f32[64,1,2560]{2,1,0:T(1,128)} %all_to_all.8), calls=%async_computation | async-start | bytes 1310720 | tf_op jit(solution)/shard_map/all_to_all | solution.py:128
  29.1 22.7 %copy-start.2 = (f32[5,32,16,1]{3,2,1,0:T(8,128)}, f32[5,32,16,1]{3,2,1,0:T(8,128)S(1)}, u32[]{:S(2)}) copy-start(f32[5,32,16,1]{3,2,1,0:T(8,128)S(1)} %copy.37) | copy-start | bytes 30724
  30.7 12.4 %copy-start.3 = (f32[5,32,16,1]{3,2,1,0:T(8,128)S(1)}, f32[5,32,16,1]{3,2,1,0:T(8,128)}, u32[]{:S(2)}) copy-start(f32[5,32,16,1]{3,2,1,0:T(8,128)} %copy.39) | copy-start | bytes 30724
  33.2 8.4 %collective-permute-start.2 = (f32[5,32,1,130]{3,2,1,0:T(1,128)S(1)}, f32[5,32,1,130]{3,2,1,0:T(1,128)S(1)}, u32[]{:S(2)}, u32[]{:S(2)}) collective-permute-start(f32[5,32,1,130]{3,2,1,0:T(1,128)S(1)} %get-tuple-element.80), channel_id=1, source_target_pairs={{4,0},{8,4},{12,8},{16,12},{20,16},{24,20},{28,24},{32,28},{36,32}... | collective-permute-start | bytes 249608 | tf_op jit(solution)/shard_map/ppermute | solution.py:27
  35.2 7.9 %collective-permute-start.3 = (f32[5,32,1,130]{3,2,1,0:T(1,128)S(1)}, f32[5,32,1,130]{3,2,1,0:T(1,128)S(1)}, u32[]{:S(2)}, u32[]{:S(2)}) collective-permute-start(f32[5,32,1,130]{3,2,1,0:T(1,128)S(1)} %get-tuple-element.79), channel_id=1, source_target_pairs={{0,4},{4,8},{8,12},{12,16},{16,20},{20,24},{24,28},{28,32},{32,36}... | collective-permute-start | bytes 249608 | tf_op jit(solution)/shard_map/ppermute | solution.py:24
  43.2 7.3 %collective-permute-start.4 = (f32[5,1,18,130]{3,2,1,0:T(8,128)S(1)}, f32[5,1,18,130]{3,2,1,0:T(8,128)S(1)}, u32[]{:S(2)}, u32[]{:S(2)}) collective-permute-start(f32[5,1,18,130]{3,2,1,0:T(8,128)S(1)} %get-tuple-element.72), channel_id=1, source_target_pairs={{1,0},{2,1},{3,2},{5,4},{6,5},{7,6},{9,8},{10,9},{11,10},{13,12},{... | collective-permute-start | bytes 140408 | tf_op jit(solution)/shard_map/ppermute | solution.py:27
  44.5 7.2 %collective-permute-start.5 = (f32[5,1,18,130]{3,2,1,0:T(8,128)S(1)}, f32[5,1,18,130]{3,2,1,0:T(8,128)S(1)}, u32[]{:S(2)}, u32[]{:S(2)}) collective-permute-start(f32[5,1,18,130]{3,2,1,0:T(8,128)S(1)} %get-tuple-element.71), channel_id=1, source_target_pairs={{0,1},{1,2},{2,3},{4,5},{5,6},{6,7},{8,9},{9,10},{10,11},{12,13},{... | collective-permute-start | bytes 140408 | tf_op jit(solution)/shard_map/ppermute | solution.py:24
  50.4 4.5 %copy-start.6 = (f32[32,16,128]{2,1,0:T(8,128)S(1)}, f32[32,16,128]{2,1,0:T(8,128)}, u32[]{:S(2)}) copy-start(f32[32,16,128]{2,1,0:T(8,128)} %param.14) | copy-start | bytes 786436
  50.5 4.4 %copy-start.8 = (f32[5,1,18,130]{3,2,1,0:T(8,128)}, f32[5,1,18,130]{3,2,1,0:T(8,128)S(1)}, u32[]{:S(2)}) copy-start(f32[5,1,18,130]{3,2,1,0:T(8,128)S(1)} %collective-permute-done.4) | copy-start | bytes 140404
  51.7 3.2 %copy-start.9 = (f32[5,1,18,130]{3,2,1,0:T(8,128)}, f32[5,1,18,130]{3,2,1,0:T(8,128)S(1)}, u32[]{:S(2)}) copy-start(f32[5,1,18,130]{3,2,1,0:T(8,128)S(1)} %collective-permute-done.5) | copy-start | bytes 140404
  61.3 32.6 %copy-start.16 = (f32[5]{0:T(128)S(1)}, f32[5]{0:T(128)}, u32[]{:S(2)}) copy-start(f32[5]{0:T(128)} %constant.116.clone) | copy-start | bytes 64
  61.4 32.6 %copy-start.15 = (f32[5]{0:T(128)S(1)}, f32[5]{0:T(128)}, u32[]{:S(2)}) copy-start(f32[5]{0:T(128)} %constant.117.clone) | copy-start | bytes 64
  103.5 9.7 %copy-start.12 = (s32[1,16,1,2048]{3,2,1,0:T(1,128)S(1)}, s32[1,16,1,2048]{3,2,1,0:T(1,128)}, u32[]{:S(2)}) copy-start(s32[1,16,1,2048]{3,2,1,0:T(1,128)} %param.19) | copy-start | bytes 393220
  105.4 7.8 %collective-permute-start.6 = (f32[5,32,16,1]{1,2,3,0:T(8,128)S(1)}, f32[5,32,16,1]{1,2,3,0:T(8,128)S(1)}, u32[]{:S(2)}, u32[]{:S(2)}) collective-permute-start(f32[5,32,16,1]{1,2,3,0:T(8,128)S(1)} %copy.44), channel_id=1, source_target_pairs={{64,0},{128,64},{192,128},{256,192},{320,256},{384,320},{448,384},... | collective-permute-start | bytes 30728 | tf_op jit(solution)/shard_map/ppermute | solution.py:27
  108.5 6.3 %collective-permute-start.7 = (f32[5,32,16,1]{1,2,3,0:T(8,128)S(1)}, f32[5,32,16,1]{1,2,3,0:T(8,128)S(1)}, u32[]{:S(2)}, u32[]{:S(2)}) collective-permute-start(f32[5,32,16,1]{1,2,3,0:T(8,128)S(1)} %copy.46), channel_id=1, source_target_pairs={{0,64},{64,128},{128,192},{192,256},{256,320},{320,384},{384,448},... | collective-permute-start | bytes 30728 | tf_op jit(solution)/shard_map/ppermute | solution.py:24
  116.4 11.6 %copy-start.5 = (f32[5,32,16,1]{3,2,1,0:T(8,128)S(1)}, f32[5,32,16,1]{3,2,1,0:T(8,128)}, u32[]{:S(2)}) copy-start(f32[5,32,16,1]{3,2,1,0:T(8,128)} %copy.47) | copy-start | bytes 30724
  119.3 8.7 %copy-start.4 = (f32[5,32,16,1]{3,2,1,0:T(8,128)S(1)}, f32[5,32,16,1]{3,2,1,0:T(8,128)}, u32[]{:S(2)}) copy-start(f32[5,32,16,1]{3,2,1,0:T(8,128)} %copy.45) | copy-start | bytes 30724
  119.3 4.9 %collective-permute-start.8 = (f32[5,32,1,130]{3,2,1,0:T(1,128)S(1)}, f32[5,32,1,130]{3,2,1,0:T(1,128)S(1)}, u32[]{:S(2)}, u32[]{:S(2)}) collective-permute-start(f32[5,32,1,130]{3,2,1,0:T(1,128)S(1)} %get-tuple-element.76), channel_id=1, source_target_pairs={{4,0},{8,4},{12,8},{16,12},{20,16},{24,20},{28,24},{32,28},{36,32}... | collective-permute-start | bytes 249608 | tf_op jit(solution)/shard_map/ppermute | solution.py:27
  121.4 6.6 %collective-permute-start.9 = (f32[5,32,1,130]{3,2,1,0:T(1,128)S(1)}, f32[5,32,1,130]{3,2,1,0:T(1,128)S(1)}, u32[]{:S(2)}, u32[]{:S(2)}) collective-permute-start(f32[5,32,1,130]{3,2,1,0:T(1,128)S(1)} %get-tuple-element.75), channel_id=1, source_target_pairs={{0,4},{4,8},{8,12},{12,16},{16,20},{20,24},{24,28},{28,32},{32,36}... | collective-permute-start | bytes 249608 | tf_op jit(solution)/shard_map/ppermute | solution.py:24
  128.2 7.4 %collective-permute-start.10 = (f32[5,1,18,130]{3,2,1,0:T(8,128)S(1)}, f32[5,1,18,130]{3,2,1,0:T(8,128)S(1)}, u32[]{:S(2)}, u32[]{:S(2)}) collective-permute-start(f32[5,1,18,130]{3,2,1,0:T(8,128)S(1)} %get-tuple-element.70), channel_id=1, source_target_pairs={{1,0},{2,1},{3,2},{5,4},{6,5},{7,6},{9,8},{10,9},{11,10},{13,12},{... | collective-permute-start | bytes 140408 | tf_op jit(solution)/shard_map/ppermute | solution.py:27
  129.5 7.4 %collective-permute-start.11 = (f32[5,1,18,130]{3,2,1,0:T(8,128)S(1)}, f32[5,1,18,130]{3,2,1,0:T(8,128)S(1)}, u32[]{:S(2)}, u32[]{:S(2)}) collective-permute-start(f32[5,1,18,130]{3,2,1,0:T(8,128)S(1)} %get-tuple-element.69), channel_id=1, source_target_pairs={{0,1},{1,2},{2,3},{4,5},{5,6},{6,7},{8,9},{9,10},{10,11},{12,13},{... | collective-permute-start | bytes 140408 | tf_op jit(solution)/shard_map/ppermute | solution.py:24
  145.4 1.1 copy-start.7
  146.4 28.6 %copy-start.10 = (f32[1,16,1,3,2048]{4,2,3,1,0:T(1,128)S(1)}, f32[1,16,1,3,2048]{4,2,3,1,0:T(1,128)}, u32[]{:S(2)}) copy-start(f32[1,16,1,3,2048]{4,2,3,1,0:T(1,128)} %param.18) | copy-start | bytes 1179652
where the time goes:
time: 264 us; the launch traced here: 263 us
  blocking collectives  125 us (47%)
  starting transfers between devices  46.3 us (18%)
  other arithmetic  36.1 us (14%)
  local copies, waits for them, and re-layouts  30.7 us (12%)
  waiting for transfers between devices  12.1 us (5%)
  matrix products  11.3 us (4%)
    psum x1, blocking collectives, on_device(): modal_force = lax.psum(modal_part, ('stream', 'vert'))  77.3 us
    psum x1, blocking collectives, on_device(): lax.psum(partial_value, 'stream').reshape(5, depth_cells, span_cells)  30.8 us
    ppermute x6, starting transfers between devices, extended(): lax.ppermute(lax.slice_in_dim(block, block.shape[dim] - width, None, axis...  23.8 us
    all_gather x1, blocking collectives, on_device(): lax.all_gather(sampled.reshape(1, 1, 1, -1), 'span', axis=1, tiled=True)  16.8 us
    all_to_all x1, starting transfers between devices, on_device(): lax.all_to_all(outgoing.reshape(tile_count, CAP * 5 * spec_cols), ('span'...  13.3 us
    gather x1, local copies, waits for them, and re-layouts, on_device(): sampled = pressure[deck_cells[0, 0, 0]]  11.8 us
    dot_general x16, matrix products, add_row(): jnp.dot(row_values, member, precision=lax.Precision.HIGHEST)  9.31 us
    ppermute x6, starting transfers between devices, extended(): lax.ppermute(lax.slice_in_dim(block, 0, width, axis=dim), axis, backward)  9.23 us
  transfers between devices with their start and end apart: 13, of which 7 were waited for; matrix products, arithmetic and copies ran while one was open for 8% of the time, Pallas kernels for 0%

commit v1 on v0

--- a/solution.py
+++ b/solution.py
@@ -162,7 +162,7 @@
     traction = rows_all[0, :, 0][:, None, :] * deck_geom[0, :, 0]
     forces = strip_forces(traction, strip_ids[0, :, 0], strip_count)
     modal_part = jnp.einsum("cj,cjm->m", forces, mode_shapes, precision=lax.Precision.HIGHEST)
-    modal_force = lax.psum(modal_part, ("stream", "vert"))
+    modal_force = lax.psum(lax.psum(modal_part, "stream"), "vert")
     return (new_fields, modal_force)
 
 

time: 264 us -> 217 us (0.82)
  the two profiles are of different devices: /device:TPU:64 before, /device:TPU:24 now
where the time goes in v1:
time: 217 us
  blocking collectives  82.1 us (38%)
  starting transfers between devices  49.6 us (23%)
  other arithmetic  36.1 us (17%)
  local copies, waits for them, and re-layouts  30.7 us (14%)
  matrix products  11.3 us (5%)
  waiting for transfers between devices  4.84 us (2%)
    psum x2, blocking collectives, on_device(): modal_force = lax.psum(lax.psum(modal_part, 'stream'), 'vert')  28.5 us
    psum x1, blocking collectives, on_device(): lax.psum(partial_value, 'stream').reshape(5, depth_cells, span_cells)  28.1 us
    all_gather x1, blocking collectives, on_device(): lax.all_gather(sampled.reshape(1, 1, 1, -1), 'span', axis=1, tiled=True)  25.6 us
    ppermute x6, starting transfers between devices, extended(): lax.ppermute(lax.slice_in_dim(block, block.shape[dim] - width, None, axis...  24.2 us
    all_to_all x1, starting transfers between devices, on_device(): lax.all_to_all(outgoing.reshape(tile_count, CAP * 5 * spec_cols), ('span'...  14.1 us
    gather x1, local copies, waits for them, and re-layouts, on_device(): sampled = pressure[deck_cells[0, 0, 0]]  11.8 us
    ppermute x6, starting transfers between devices, extended(): lax.ppermute(lax.slice_in_dim(block, 0, width, axis=dim), axis, backward)  11.3 us
    dot_general x16, matrix products, add_row(): jnp.dot(row_values, member, precision=lax.Precision.HIGHEST)  9.31 us
  transfers between devices with their start and end apart: 13, of which 5 were waited for; matrix products, arithmetic and copies ran while one was open for 10% of the time, Pallas kernels for 0%

profile of v1, /device:TPU:24, one launch (start us, length us, event | category | flops | bytes accessed | tf_op | source)
XLA Modules:
  0.0 216.7 jit_solution(1224090058101289588)
XLA Ops:
  0.6 2.2 fusion.52
  3.4 2.4 %collective-permute-start = (f32[5,32,16,1]{1,2,3,0:T(8,128)S(1)}, f32[5,32,16,1]{1,2,3,0:T(8,128)S(1)}, u32[]{:S(2)}, u32[]{:S(2)}) collective-permute-start(f32[5,32,16,1]{1,2,3,0:T(8,128)S(1)} %copy.55), channel_id=1, source_target_pairs={{64,0},{128,64},{192,128},{256,192},{320,256},{384,320},{448,384},... | collective-permute-start | bytes 30728 | tf_op jit(solution)/shard_map/ppermute | solution.py:27
  6.4 4.7 %collective-permute-start.1 = (f32[5,32,16,1]{1,2,3,0:T(8,128)S(1)}, f32[5,32,16,1]{1,2,3,0:T(8,128)S(1)}, u32[]{:S(2)}, u32[]{:S(2)}) collective-permute-start(f32[5,32,16,1]{1,2,3,0:T(8,128)S(1)} %copy.56), channel_id=1, source_target_pairs={{0,64},{64,128},{128,192},{192,256},{256,320},{320,384},{384,448},... | collective-permute-start | bytes 30728 | tf_op jit(solution)/shard_map/ppermute | solution.py:24
  11.9 1.5 all_to_all.8
  13.5 14.1 %all-to-all-start = ((f32[64,1,2560]{2,1,0:T(1,128)}), f32[64,1,2560]{2,1,0:T(1,128)}, u32[]{:S(2)}, u32[]{:S(2)}) async-start(f32[64,1,2560]{2,1,0:T(1,128)} %all_to_all.8), calls=%async_computation | async-start | bytes 1310720 | tf_op jit(solution)/shard_map/all_to_all | solution.py:128
  27.6 0.9 bitcast_multiply_fusion.6
  28.8 1.8 fusion.46
  31.2 1.6 copy.39
  32.8 2.5 %pad_maximum_fusion.39 = (f32[5,32,1,130]{3,2,1,0:T(1,128)S(1)}, f32[5,32,1,130]{3,2,1,0:T(1,128)S(1)}) fusion(f32[5,32,16,1]{3,2,1,0:T(8,128)S(1)} %copy.37, f32[5,32,16,128]{3,2,1,0:T(8,128)S(1)} %copy-done.1, f32[5,32,16,1]{3,2,1,0:T(8,128)} %copy.39), kind=kLoop, calls=%fused_computation.121 | loop fusion | flops 83200 | bytes 1497600 | tf_op jit(solution)/shard_map/concatenate | solution.py:28
  35.3 1.3 collective-permute-start.2
  36.6 3.0 %collective-permute-start.3 = (f32[5,32,1,130]{3,2,1,0:T(1,128)S(1)}, f32[5,32,1,130]{3,2,1,0:T(1,128)S(1)}, u32[]{:S(2)}, u32[]{:S(2)}) collective-permute-start(f32[5,32,1,130]{3,2,1,0:T(1,128)S(1)} %get-tuple-element.79), channel_id=1, source_target_pairs={{0,4},{4,8},{8,12},{12,16},{16,20},{20,24},{24,28},{28,32},{32,36}... | collective-permute-start | bytes 249608 | tf_op jit(solution)/shard_map/ppermute | solution.py:24
  39.7 1.0 collective-permute-done.3
  40.8 1.3 collective-permute-start.4
  42.1 4.7 %collective-permute-start.5 = (f32[5,1,18,130]{3,2,1,0:T(8,128)S(1)}, f32[5,1,18,130]{3,2,1,0:T(8,128)S(1)}, u32[]{:S(2)}, u32[]{:S(2)}) collective-permute-start(f32[5,1,18,130]{3,2,1,0:T(8,128)S(1)} %get-tuple-element.71), channel_id=1, source_target_pairs={{0,1},{1,2},{2,3},{4,5},{5,6},{6,7},{8,9},{9,10},{10,11},{12,13},{... | collective-permute-start | bytes 140408 | tf_op jit(solution)/shard_map/ppermute | solution.py:24
  46.9 1.1 broadcast_multiply_fusion.4
  48.0 1.1 collective-permute-done.5
  49.1 3.2 %broadcast_multiply_fusion.3 = (f32[5,32,16,128]{3,2,1,0:T(8,128)S(1)}, f32[5,32,16,128]{3,2,1,0:T(8,128)S(1)}) fusion(f32[5,1,18,130]{3,2,1,0:T(8,128)S(1)} %collective-permute-done.4, f32[5,32,1,130]{3,2,1,0:T(1,128)S(1)} %collective-permute-done.2, f32[5,32,16,1]{3,2,1,0:T(8,128)S(1)} %copy.37, f32[5,32,16,128]{3,2,1,0:T(8,128)S(1)} %copy-done.1, ...), kind=kLoop, calls=%fused_computation.50 | loop fusion | flops 5242880 | bytes 4212640 | tf_op jit(solution)/shard_map/mul | solution.py:59
  52.3 0.7 fusion.40
  53.0 0.8 fusion.36
  53.8 0.8 fusion.32
  54.6 0.8 fusion.27
  56.1 2.6 %reduce = f32[64,2560]{1,0:T(8,128)S(1)} reduce(f32[64,1,2560]{2,1,0:T(1,128)} %all-to-all-done, f32[]{:T(128)} %constant.123), dimensions={1}, to_apply=%all_to_all.7.reduce_sub_computation | reduce | bytes 1310724 | tf_op jit(solution)/shard_map/all_to_all | solution.py:128
  58.9 1.5 fusion.3
  60.5 28.1 %psum.21 = f32[5,32,16]{2,1,0:T(8,128)S(1)} all-reduce(f32[5,32,16]{2,1,0:T(8,128)S(1)} %reshape.200), channel_id=1, replica_groups=mesh['stream'=8,'span'=16,'vert'=4] {'stream'}, use_global_device_ids=true, to_apply=%region_3.4 | all-reduce | flops 2560 | bytes 20480 | tf_op jit(solution)/shard_map/psum | solution.py:144
  88.6 7.5 %multiply_add_fusion = f32[5,32,16,128]{3,2,1,0:T(8,128)S(1)} fusion(f32[5,32,16,128]{3,2,1,0:T(8,128)S(1)} %copy-done.1, f32[5,32,16,128]{3,2,1,0:T(8,128)} %broadcast_dynamic-update-slice_fusion.1, f32[5,32,16]{2,1,0:T(8,128)S(1)} %broadcast_add_fusion.1, f32[128]{0:T(128)S(1)} %compare_select_fusion.1, f32[32,16,128]{2,1,0:T(8,128)} %get-tuple-element.87, ...), kind=kLoop, calls=%fused_computation.45 | loop fusion | flops 13434880 | bytes 5009844 | tf_op jit(solution)/shard_map/add | solution.py:155
  96.1 1.9 fusion.51
  98.1 1.9 copy.44
  100.0 3.6 %collective-permute-start.6 = (f32[5,32,16,1]{1,2,3,0:T(8,128)S(1)}, f32[5,32,16,1]{1,2,3,0:T(8,128)S(1)}, u32[]{:S(2)}, u32[]{:S(2)}) collective-permute-start(f32[5,32,16,1]{1,2,3,0:T(8,128)S(1)} %copy.44), channel_id=1, source_target_pairs={{64,0},{128,64},{192,128},{256,192},{320,256},{384,320},{448,384},... | collective-permute-start | bytes 30728 | tf_op jit(solution)/shard_map/ppermute | solution.py:27
  103.6 1.9 copy.46
  105.5 3.4 %collective-permute-start.7 = (f32[5,32,16,1]{1,2,3,0:T(8,128)S(1)}, f32[5,32,16,1]{1,2,3,0:T(8,128)S(1)}, u32[]{:S(2)}, u32[]{:S(2)}) collective-permute-start(f32[5,32,16,1]{1,2,3,0:T(8,128)S(1)} %copy.46), channel_id=1, source_target_pairs={{0,64},{64,128},{128,192},{192,256},{256,320},{320,384},{384,448},... | collective-permute-start | bytes 30728 | tf_op jit(solution)/shard_map/ppermute | solution.py:24
  109.0 1.6 copy.45
  110.6 0.7 collective-permute-done.7
  111.4 1.6 copy.47
  113.0 2.9 %pad_maximum_fusion.36 = (f32[5,32,1,130]{3,2,1,0:T(1,128)S(1)}, f32[5,32,1,130]{3,2,1,0:T(1,128)S(1)}) fusion(f32[5,32,16,1]{3,2,1,0:T(8,128)} %copy.45, f32[5,32,16,128]{3,2,1,0:T(8,128)S(1)} %multiply_add_fusion, f32[5,32,16,1]{3,2,1,0:T(8,128)} %copy.47), kind=kLoop, calls=%fused_computation.118 | loop fusion | flops 83200 | bytes 1497600 | tf_op jit(solution)/shard_map/concatenate | solution.py:28
  115.9 1.4 collective-permute-start.8
  117.3 3.3 %collective-permute-start.9 = (f32[5,32,1,130]{3,2,1,0:T(1,128)S(1)}, f32[5,32,1,130]{3,2,1,0:T(1,128)S(1)}, u32[]{:S(2)}, u32[]{:S(2)}) collective-permute-start(f32[5,32,1,130]{3,2,1,0:T(1,128)S(1)} %get-tuple-element.75), channel_id=1, source_target_pairs={{0,4},{4,8},{8,12},{12,16},{16,20},{20,24},{24,28},{28,32},{32,36}... | collective-permute-start | bytes 249608 | tf_op jit(solution)/shard_map/ppermute | solution.py:24
  121.5 1.3 collective-permute-start.10
  122.8 5.1 %collective-permute-start.11 = (f32[5,1,18,130]{3,2,1,0:T(8,128)S(1)}, f32[5,1,18,130]{3,2,1,0:T(8,128)S(1)}, u32[]{:S(2)}, u32[]{:S(2)}) collective-permute-start(f32[5,1,18,130]{3,2,1,0:T(8,128)S(1)} %get-tuple-element.69), channel_id=1, source_target_pairs={{0,1},{1,2},{2,3},{4,5},{5,6},{6,7},{8,9},{9,10},{10,11},{12,13},{... | collective-permute-start | bytes 140408 | tf_op jit(solution)/shard_map/ppermute | solution.py:24
  127.9 1.1 broadcast_multiply_fusion.1
  129.0 1.3 collective-permute-done.11
  130.3 3.1 %broadcast_multiply_fusion = (f32[5,32,16,128]{3,2,1,0:T(8,128)S(1)}, f32[5,32,16,128]{3,2,1,0:T(8,128)S(1)}) fusion(f32[5,1,18,130]{3,2,1,0:T(8,128)S(1)} %collective-permute-done.10, f32[5,32,1,130]{3,2,1,0:T(1,128)S(1)} %collective-permute-done.8, f32[5,32,16,1]{3,2,1,0:T(8,128)S(1)} %copy-done.4, f32[5,32,16,128]{3,2,1,0:T(8,128)S(1)} %multiply_add_fusion, ...), kind=kLoop, calls=%fused_computation.47 | loop fusion | flops 5242880 | bytes 4212640 | tf_op jit(solution)/shard_map/mul | solution.py:59
  133.8 5.0 %add_multiply_fusion = f32[5,32,16,128]{3,2,1,0:T(8,128)S(1)} fusion(f32[5,32,16,128]{3,2,1,0:T(8,128)S(1)} %broadcast_dynamic-update-slice_fusion, f32[5,32,16,128]{3,2,1,0:T(8,128)S(1)} %multiply_add_fusion, f32[5,32,16,128]{3,2,1,0:T(8,128)S(1)} %copy-done.1, f32[32,16,128]{2,1,0:T(8,128)S(1)} %get-tuple-element.82, ...), kind=kLoop, calls=%fused_computation.44 | loop fusion | flops 14090240 | bytes 6320564 | tf_op jit(solution)/shard_map/mul | solution.py:157
  138.8 1.0 copy-done.7
  139.9 11.8 %gather_fusion = f32[2048]{0:T(1024)S(1)} fusion(f32[65536]{0:T(1024)S(1)} %bitcast.150, s32[2048]{0:T(1024)S(1)} %broadcast_clamp_fusion), kind=kCustom, calls=%fused_computation | custom fusion | bytes 24576 | tf_op jit(solution)/shard_map/gather | solution.py:159
  151.7 25.6 %all-gather = f32[32768]{0:T(1024)S(1)} all-gather(f32[2048]{0:T(1024)S(1)} %gather_fusion), channel_id=2, replica_groups=mesh['stream'=8,'span'=16,'vert'=4] {'span'}, dimensions={0}, use_global_device_ids=true | all-gather | bytes 139264 | tf_op jit(solution)/shard_map/all_gather | solution.py:161
  177.4 10.6 %while.11 = (s32[]{:T(128)}, f32[3,64]{1,0:T(4,128)S(1)}, f32[16,3,2048]{2,0,1:T(8,128)S(1)}, s32[16,2048]{1,0:T(8,128)S(1)}, s32[]{:T(128)}, /*index=5*/s32[]{:T(128)}) while((s32[]{:T(128)}, f32[3,64]{1,0:T(4,128)S(1)}, f32[16,3,2048]{2,0,1:T(8,128)S(1)}, s32[16,2048]{1,0:T(8,128)S(1)}, s32[]{:T(128)}, /*index=5*/s32[]{:T(128)}) %tuple.46), condition=%wide.region_5.6_spmd.clone, body=%wide.region_4.5_spmd.clone.sunk | while | flops 4850051 | bytes 99927 | solution.py:104
  188.2 15.7 %psum.22 = f32[32]{0:T(128)S(1)} all-reduce(f32[32]{0:T(128)S(1)} %convolution_bitcast_fusion), channel_id=1, replica_groups=mesh['stream'=8,'span'=16,'vert'=4] {'stream'}, use_global_device_ids=true, to_apply=%region_6.7 | all-reduce | flops 32 | bytes 256 | tf_op jit(solution)/shard_map/psum | solution.py:165
  203.9 12.8 %psum.23 = f32[32]{0:T(128)} all-reduce(f32[32]{0:T(128)S(1)} %psum.22), channel_id=1, replica_groups=mesh['stream'=8,'span'=16,'vert'=4] {'vert'}, use_global_device_ids=true, to_apply=%region_7.8 | all-reduce | flops 32 | bytes 256 | tf_op jit(solution)/shard_map/psum | solution.py:165
  (129 shorter events, 15.7 us)
Async XLA Ops:
  0.6 187.4 %copy-start = (f32[3,64,32]{1,2,0:T(8,128)S(1)}, f32[3,64,32]{1,2,0:T(8,128)}, u32[]{:S(2)}) copy-start(f32[3,64,32]{1,2,0:T(8,128)} %param.20) | copy-start | bytes 73732
  2.8 8.3 %copy-start.14 = (s32[64,1]{0,1:T(1,128)S(1)}, s32[64,1]{0,1:T(1,128)}, u32[]{:S(2)}) copy-start(s32[64,1]{0,1:T(1,128)} %param.16) | copy-start | bytes 772
  2.8 8.7 %copy-start.11 = (f32[64,5,256]{2,0,1:T(8,128)S(1)}, f32[64,5,256]{2,0,1:T(8,128)}, u32[]{:S(2)}) copy-start(f32[64,5,256]{2,0,1:T(8,128)} %param.15) | copy-start | bytes 983044
  3.4 27.1 %collective-permute-start = (f32[5,32,16,1]{1,2,3,0:T(8,128)S(1)}, f32[5,32,16,1]{1,2,3,0:T(8,128)S(1)}, u32[]{:S(2)}, u32[]{:S(2)}) collective-permute-start(f32[5,32,16,1]{1,2,3,0:T(8,128)S(1)} %copy.55), channel_id=1, source_target_pairs={{64,0},{128,64},{192,128},{256,192},{320,256},{384,320},{448,384},... | collective-permute-start | bytes 30728 | tf_op jit(solution)/shard_map/ppermute | solution.py:27
  6.4 24.8 %collective-permute-start.1 = (f32[5,32,16,1]{1,2,3,0:T(8,128)S(1)}, f32[5,32,16,1]{1,2,3,0:T(8,128)S(1)}, u32[]{:S(2)}, u32[]{:S(2)}) collective-permute-start(f32[5,32,16,1]{1,2,3,0:T(8,128)S(1)} %copy.56), channel_id=1, source_target_pairs={{0,64},{64,128},{128,192},{192,256},{256,320},{320,384},{384,448},... | collective-permute-start | bytes 30728 | tf_op jit(solution)/shard_map/ppermute | solution.py:24
  11.9 15.7 %copy-start.1 = (f32[5,32,16,128]{3,2,1,0:T(8,128)S(1)}, f32[5,32,16,128]{3,2,1,0:T(8,128)}, u32[]{:S(2)}) copy-start(f32[5,32,16,128]{3,2,1,0:T(8,128)} %param.13) | copy-start | bytes 3932164
  13.5 15.1 %copy-start.13 = (s32[1,1,1,2048]{3,2,1,0:T(1,128)S(1)}, s32[1,1,1,2048]{3,2,1,0:T(1,128)}, u32[]{:S(2)}) copy-start(s32[1,1,1,2048]{3,2,1,0:T(1,128)} %param.17) | copy-start | bytes 24580
  13.5 42.6 %all-to-all-start = ((f32[64,1,2560]{2,1,0:T(1,128)}), f32[64,1,2560]{2,1,0:T(1,128)}, u32[]{:S(2)}, u32[]{:S(2)}) async-start(f32[64,1,2560]{2,1,0:T(1,128)} %all_to_all.8), calls=%async_computation | async-start | bytes 1310720 | tf_op jit(solution)/shard_map/all_to_all | solution.py:128
  31.2 17.9 %copy-start.2 = (f32[5,32,16,1]{3,2,1,0:T(8,128)}, f32[5,32,16,1]{3,2,1,0:T(8,128)S(1)}, u32[]{:S(2)}) copy-start(f32[5,32,16,1]{3,2,1,0:T(8,128)S(1)} %copy.37) | copy-start | bytes 30724
  32.8 7.8 %copy-start.3 = (f32[5,32,16,1]{3,2,1,0:T(8,128)S(1)}, f32[5,32,16,1]{3,2,1,0:T(8,128)}, u32[]{:S(2)}) copy-start(f32[5,32,16,1]{3,2,1,0:T(8,128)} %copy.39) | copy-start | bytes 30724
  35.3 4.4 %collective-permute-start.2 = (f32[5,32,1,130]{3,2,1,0:T(1,128)S(1)}, f32[5,32,1,130]{3,2,1,0:T(1,128)S(1)}, u32[]{:S(2)}, u32[]{:S(2)}) collective-permute-start(f32[5,32,1,130]{3,2,1,0:T(1,128)S(1)} %get-tuple-element.80), channel_id=1, source_target_pairs={{4,0},{8,4},{12,8},{16,12},{20,16},{24,20},{28,24},{32,28},{36,32}... | collective-permute-start | bytes 249608 | tf_op jit(solution)/shard_map/ppermute | solution.py:27
  36.6 4.0 %collective-permute-start.3 = (f32[5,32,1,130]{3,2,1,0:T(1,128)S(1)}, f32[5,32,1,130]{3,2,1,0:T(1,128)S(1)}, u32[]{:S(2)}, u32[]{:S(2)}) collective-permute-start(f32[5,32,1,130]{3,2,1,0:T(1,128)S(1)} %get-tuple-element.79), channel_id=1, source_target_pairs={{0,4},{4,8},{8,12},{12,16},{16,20},{20,24},{24,28},{28,32},{32,36}... | collective-permute-start | bytes 249608 | tf_op jit(solution)/shard_map/ppermute | solution.py:24
  40.8 7.2 %collective-permute-start.4 = (f32[5,1,18,130]{3,2,1,0:T(8,128)S(1)}, f32[5,1,18,130]{3,2,1,0:T(8,128)S(1)}, u32[]{:S(2)}, u32[]{:S(2)}) collective-permute-start(f32[5,1,18,130]{3,2,1,0:T(8,128)S(1)} %get-tuple-element.72), channel_id=1, source_target_pairs={{1,0},{2,1},{3,2},{5,4},{6,5},{7,6},{9,8},{10,9},{11,10},{13,12},{... | collective-permute-start | bytes 140408 | tf_op jit(solution)/shard_map/ppermute | solution.py:27
  42.1 7.0 %collective-permute-start.5 = (f32[5,1,18,130]{3,2,1,0:T(8,128)S(1)}, f32[5,1,18,130]{3,2,1,0:T(8,128)S(1)}, u32[]{:S(2)}, u32[]{:S(2)}) collective-permute-start(f32[5,1,18,130]{3,2,1,0:T(8,128)S(1)} %get-tuple-element.71), channel_id=1, source_target_pairs={{0,1},{1,2},{2,3},{4,5},{5,6},{6,7},{8,9},{9,10},{10,11},{12,13},{... | collective-permute-start | bytes 140408 | tf_op jit(solution)/shard_map/ppermute | solution.py:24
  48.0 4.3 %copy-start.6 = (f32[32,16,128]{2,1,0:T(8,128)S(1)}, f32[32,16,128]{2,1,0:T(8,128)}, u32[]{:S(2)}) copy-start(f32[32,16,128]{2,1,0:T(8,128)} %param.14) | copy-start | bytes 786436
  48.0 4.3 %copy-start.8 = (f32[5,1,18,130]{3,2,1,0:T(8,128)}, f32[5,1,18,130]{3,2,1,0:T(8,128)S(1)}, u32[]{:S(2)}) copy-start(f32[5,1,18,130]{3,2,1,0:T(8,128)S(1)} %collective-permute-done.4) | copy-start | bytes 140404
  49.1 3.2 %copy-start.9 = (f32[5,1,18,130]{3,2,1,0:T(8,128)}, f32[5,1,18,130]{3,2,1,0:T(8,128)S(1)}, u32[]{:S(2)}) copy-start(f32[5,1,18,130]{3,2,1,0:T(8,128)S(1)} %collective-permute-done.5) | copy-start | bytes 140404
  58.7 29.8 %copy-start.16 = (f32[5]{0:T(128)S(1)}, f32[5]{0:T(128)}, u32[]{:S(2)}) copy-start(f32[5]{0:T(128)} %constant.116.clone) | copy-start | bytes 64
  58.7 29.9 %copy-start.15 = (f32[5]{0:T(128)S(1)}, f32[5]{0:T(128)}, u32[]{:S(2)}) copy-start(f32[5]{0:T(128)} %constant.117.clone) | copy-start | bytes 64
  98.1 10.9 %copy-start.12 = (s32[1,16,1,2048]{3,2,1,0:T(1,128)S(1)}, s32[1,16,1,2048]{3,2,1,0:T(1,128)}, u32[]{:S(2)}) copy-start(s32[1,16,1,2048]{3,2,1,0:T(1,128)} %param.19) | copy-start | bytes 393220
  100.0 9.0 %collective-permute-start.6 = (f32[5,32,16,1]{1,2,3,0:T(8,128)S(1)}, f32[5,32,16,1]{1,2,3,0:T(8,128)S(1)}, u32[]{:S(2)}, u32[]{:S(2)}) collective-permute-start(f32[5,32,16,1]{1,2,3,0:T(8,128)S(1)} %copy.44), channel_id=1, source_target_pairs={{64,0},{128,64},{192,128},{256,192},{320,256},{384,320},{448,384},... | collective-permute-start | bytes 30728 | tf_op jit(solution)/shard_map/ppermute | solution.py:27
  105.5 5.9 %collective-permute-start.7 = (f32[5,32,16,1]{1,2,3,0:T(8,128)S(1)}, f32[5,32,16,1]{1,2,3,0:T(8,128)S(1)}, u32[]{:S(2)}, u32[]{:S(2)}) collective-permute-start(f32[5,32,16,1]{1,2,3,0:T(8,128)S(1)} %copy.46), channel_id=1, source_target_pairs={{0,64},{64,128},{128,192},{192,256},{256,320},{320,384},{384,448},... | collective-permute-start | bytes 30728 | tf_op jit(solution)/shard_map/ppermute | solution.py:24
  113.0 8.4 %copy-start.5 = (f32[5,32,16,1]{3,2,1,0:T(8,128)S(1)}, f32[5,32,16,1]{3,2,1,0:T(8,128)}, u32[]{:S(2)}) copy-start(f32[5,32,16,1]{3,2,1,0:T(8,128)} %copy.47) | copy-start | bytes 30724
  115.9 5.5 %copy-start.4 = (f32[5,32,16,1]{3,2,1,0:T(8,128)S(1)}, f32[5,32,16,1]{3,2,1,0:T(8,128)}, u32[]{:S(2)}) copy-start(f32[5,32,16,1]{3,2,1,0:T(8,128)} %copy.45) | copy-start | bytes 30724
  115.9 4.8 %collective-permute-start.8 = (f32[5,32,1,130]{3,2,1,0:T(1,128)S(1)}, f32[5,32,1,130]{3,2,1,0:T(1,128)S(1)}, u32[]{:S(2)}, u32[]{:S(2)}) collective-permute-start(f32[5,32,1,130]{3,2,1,0:T(1,128)S(1)} %get-tuple-element.76), channel_id=1, source_target_pairs={{4,0},{8,4},{12,8},{16,12},{20,16},{24,20},{28,24},{32,28},{36,32}... | collective-permute-start | bytes 249608 | tf_op jit(solution)/shard_map/ppermute | solution.py:27
  117.3 4.0 %collective-permute-start.9 = (f32[5,32,1,130]{3,2,1,0:T(1,128)S(1)}, f32[5,32,1,130]{3,2,1,0:T(1,128)S(1)}, u32[]{:S(2)}, u32[]{:S(2)}) collective-permute-start(f32[5,32,1,130]{3,2,1,0:T(1,128)S(1)} %get-tuple-element.75), channel_id=1, source_target_pairs={{0,4},{4,8},{8,12},{12,16},{16,20},{20,24},{24,28},{28,32},{32,36}... | collective-permute-start | bytes 249608 | tf_op jit(solution)/shard_map/ppermute | solution.py:24
  121.5 7.5 %collective-permute-start.10 = (f32[5,1,18,130]{3,2,1,0:T(8,128)S(1)}, f32[5,1,18,130]{3,2,1,0:T(8,128)S(1)}, u32[]{:S(2)}, u32[]{:S(2)}) collective-permute-start(f32[5,1,18,130]{3,2,1,0:T(8,128)S(1)} %get-tuple-element.70), channel_id=1, source_target_pairs={{1,0},{2,1},{3,2},{5,4},{6,5},{7,6},{9,8},{10,9},{11,10},{13,12},{... | collective-permute-start | bytes 140408 | tf_op jit(solution)/shard_map/ppermute | solution.py:27
  122.8 7.5 %collective-permute-start.11 = (f32[5,1,18,130]{3,2,1,0:T(8,128)S(1)}, f32[5,1,18,130]{3,2,1,0:T(8,128)S(1)}, u32[]{:S(2)}, u32[]{:S(2)}) collective-permute-start(f32[5,1,18,130]{3,2,1,0:T(8,128)S(1)} %get-tuple-element.69), channel_id=1, source_target_pairs={{0,1},{1,2},{2,3},{4,5},{5,6},{6,7},{8,9},{9,10},{10,11},{12,13},{... | collective-permute-start | bytes 140408 | tf_op jit(solution)/shard_map/ppermute | solution.py:24
  138.8 1.1 copy-start.7
  139.9 37.4 %copy-start.10 = (f32[1,16,1,3,2048]{4,2,3,1,0:T(1,128)S(1)}, f32[1,16,1,3,2048]{4,2,3,1,0:T(1,128)}, u32[]{:S(2)}) copy-start(f32[1,16,1,3,2048]{4,2,3,1,0:T(1,128)} %param.18) | copy-start | bytes 1179652
